TPU v7x, 512 devices: a whole 4x8x8 slice. The times are simulated.
512 devices in a mesh: ctx: 64 (over z_lo, y, core), head: 8 (over x, z_hi).
Axes of the slice: x: 4, y: 8, z: 8 (z_hi: 2, z_lo: 4; z = z_hi * 4 + z_lo), core: 2. Of those that a mesh axis runs over, the one named last changes fastest.
Arguments:
- tokens: bfloat16 [32768, 3840], P('ctx', 'head'), may hold values from -18 to 18
- w_query: bfloat16 [3840, 4096], P('ctx', 'head'), may hold values from -0.09375 to 0.09375
- key_matrix: bfloat16 [3840, 2048], P('ctx', 'head'), may hold values from -0.09375 to 0.09375
- value_matrix: bfloat16 [3840, 2048], P('ctx', 'head'), may hold values from -0.09375 to 0.09375
- d_attended: bfloat16 [32768, 4096], P('ctx', 'head'), may hold values from -6 to 6
- doc_lengths: int32 [32], replicated, may hold values from 1 to 2048, 32768 in all
Outputs:
- attended: bfloat16 [32768, 4096], P('ctx', 'head')
- key_grad: bfloat16 [32768, 2048], P('ctx', 'head')
Inputs may be any that keep to these rules, and one draw needn't show every extreme that they name: `doc_lengths`: the documents lie end to end from position 0 and fill all 32768 positions.
All inputs are finite; a program needn't handle non-finite values.
Results may differ from a plain program's by a relative error of at most 0.012.
The roundings to bfloat16 on the way count: a program that leaves them out, or rounds other values in their place, can miss the bound.
Values may be sent and summed in bfloat16 or wider, within the bound.
No kernel may reach another device: no remote copies, remote signals or barrier semaphores. Data moves between devices by JAX's collectives and lax.ppermute only.
A program may use at most 64 MiB of HBM per device.

v0:
```python
import jax
import jax.numpy as jnp
from jax import lax
from jax.sharding import PartitionSpec as P

HEAD_SIZE = 256
WINDOW = 1024


def from_behind(block, axis, distance):
    devices = range(lax.axis_size(axis))
    route = [(i - distance, i) for i in devices if i - distance in devices]
    return lax.ppermute(block, axis, route)


def doc_begin(positions, doc_start):
    inside = doc_start[None, :] <= positions[:, None]
    return jnp.max(jnp.where(inside, doc_start[None, :], 0), axis=1)


def add_rows(features, piece):
    return jnp.dot(features, piece, preferred_element_type=jnp.float32)


def attend_local(query, key_ext, value_ext, grad_rows, leading_row, doc_start, kv_heads):
    rows = query.shape[0]
    window_length = key_ext.shape[0]
    width = key_ext.shape[1] // kv_heads
    group = query.shape[1] // (kv_heads * width)
    query_pos = leading_row + jnp.arange(rows, dtype=jnp.int32)
    key_pos = leading_row - (window_length - rows) + jnp.arange(window_length, dtype=jnp.int32)
    begins = doc_begin(query_pos, doc_start)
    allowed = (
        (key_pos[None, :] >= begins[:, None])
        & (key_pos[None, :] <= query_pos[:, None])
        & (key_pos[None, :] > query_pos[:, None] - WINDOW)
    )
    query_four = query.reshape(rows, kv_heads, group, width)
    grad_four = grad_rows.reshape(rows, kv_heads, group, width)
    key_three = key_ext.reshape(window_length, kv_heads, width)
    value_three = value_ext.reshape(window_length, kv_heads, width)
    scores = jnp.einsum("tgeh,sgh->gets", query_four, key_three, preferred_element_type=jnp.float32)
    scores = jnp.where(allowed[None, None], scores, -1e30)
    peak = jnp.max(scores, axis=-1, keepdims=True)
    expo = jnp.exp(scores - peak)
    probs = expo / jnp.sum(expo, axis=-1, keepdims=True)
    probs_low = probs.astype(jnp.bfloat16)
    attended = jnp.einsum(
        "gets,sgh->tgeh", probs_low, value_three, preferred_element_type=jnp.float32
    )
    attended = attended.astype(jnp.bfloat16).reshape(rows, kv_heads * group * width)
    dprob = jnp.einsum("tgeh,sgh->gets", grad_four, value_three, preferred_element_type=jnp.float32)
    delta = jnp.sum(probs * dprob, axis=-1, keepdims=True)
    dscore = (probs * (dprob - delta)).astype(jnp.bfloat16)
    key_part = jnp.einsum("gets,tgeh->sgh", dscore, query_four, preferred_element_type=jnp.float32)
    return (attended, key_part.reshape(window_length, kv_heads * width))


def local(tokens, w_query, key_matrix, value_matrix, d_attended, doc_lengths):
    features = lax.all_gather(tokens, "head", axis=1, tiled=True)
    rows_here = features.shape[0]
    kv_width = key_matrix.shape[1]
    kv_heads = kv_width // HEAD_SIZE

    def add_one(piece):
        return add_rows(features, piece)

    query_sum = add_one(lax.all_gather(w_query, "ctx", axis=0, tiled=True))
    key_sum = add_one(lax.all_gather(key_matrix, "ctx", axis=0, tiled=True))
    value_sum = add_one(lax.all_gather(value_matrix, "ctx", axis=0, tiled=True))
    query = (query_sum * 0.0625).astype(jnp.bfloat16)
    joined = jnp.concatenate([key_sum.astype(jnp.bfloat16), value_sum.astype(jnp.bfloat16)], axis=1)
    blocks = WINDOW // rows_here
    earlier = [from_behind(joined, "ctx", distance) for distance in range(blocks, 0, -1)]
    extended = jnp.concatenate(earlier + [joined], axis=0)
    doc_start = jnp.cumsum(doc_lengths) - doc_lengths
    leading_row = lax.axis_index("ctx") * rows_here
    attended, key_part = attend_local(
        query,
        extended[:, :kv_width],
        extended[:, kv_width:],
        d_attended,
        leading_row,
        doc_start,
        kv_heads,
    )

    def share(distance):
        begin = (blocks - distance) * rows_here
        return key_part[begin : begin + rows_here]

    key_total = share(0)
    for distance in range(1, blocks + 1):
        key_total = key_total + from_behind(share(distance), "ctx", -distance)
    key_grad = key_total.astype(jnp.bfloat16)
    return (attended, key_grad)


def solution(mesh):
    return jax.shard_map(
        local,
        mesh=mesh,
        in_specs=(
            P("ctx", "head"),
            P("ctx", "head"),
            P("ctx", "head"),
            P("ctx", "head"),
            P("ctx", "head"),
            P(),
        ),
        out_specs=(P("ctx", "head"), P("ctx", "head")),
        check_vma=False,
    )
```

profile of v0, /device:TPU:24, one launch (start us, length us, event | category | flops | bytes accessed | tf_op | source)
XLA Modules:
  0.0 539.3 jit_solution(11671990753732700113)
XLA Ops:
  7.2 0.7 all-gather.10.cloned.1.call-update
  7.9 0.7 all-gather.12.cloned.1.call-update
  8.7 0.7 all-gather.8.cloned.1.call-update
  10.0 0.7 copy.35
  11.6 119.0 %all-gather.10.cloned.1.call-done = bf16[64,60,256]{2,1,0:T(8,128)(2,1)} async-done(((bf16[1,60,256]{2,1,0:T(8,128)(2,1)}), bf16[64,60,256]{2,1,0:T(8,128)(2,1)}) %all-gather.10.cloned.1.call-update) | async-done | bytes 1966096 | tf_op jit(solution)/shard_map/all_gather | solution.py:69
  130.7 2.5 reshape.188
  133.1 115.6 %all-gather.12.cloned.1.call-done = bf16[64,60,256]{2,1,0:T(8,128)(2,1)} async-done(((bf16[1,60,256]{2,1,0:T(8,128)(2,1)}), bf16[64,60,256]{2,1,0:T(8,128)(2,1)}) %all-gather.12.cloned.1.call-update) | async-done | bytes 1966096 | tf_op jit(solution)/shard_map/all_gather | solution.py:70
  248.7 3.8 reshape.190
  252.5 108.1 %all-gather.8.cloned.1.call-done = bf16[512,3840]{0,1:T(8,128)(2,1)} async-done(((bf16[512,480]{0,1:T(8,128)(2,1)}), bf16[512,3840]{0,1:T(8,128)(2,1)}) %all-gather.8.cloned.1.call-update) | async-done | bytes 3932176 | tf_op jit(solution)/shard_map/all_gather | solution.py:60
  360.6 3.5 convolution_convert_fusion.1
  364.4 1.2 convolution_convert_fusion
  365.7 1.9 collective-permute-start.1
  367.6 4.8 collective-permute-start
  372.4 1.2 compare_and_fusion
  373.6 7.6 %collective-permute-done.1 = bf16[512,512]{0,1:T(8,128)(2,1)S(1)} collective-permute-done((bf16[512,512]{0,1:T(8,128)(2,1)S(1)}, bf16[512,512]{0,1:T(8,128)(2,1)S(1)}, u32[]{:S(2)}, u32[]{:S(2)}) %collective-permute-start.1) | collective-permute-done | bytes 524320 | tf_op jit(solution)/shard_map/ppermute | solution.py:13
  381.3 6.2 %collective-permute-done = bf16[512,512]{0,1:T(8,128)(2,1)S(1)} collective-permute-done((bf16[512,512]{0,1:T(8,128)(2,1)S(1)}, bf16[512,512]{0,1:T(8,128)(2,1)S(1)}, u32[]{:S(2)}, u32[]{:S(2)}) %collective-permute-start) | collective-permute-done | bytes 524320 | tf_op jit(solution)/shard_map/ppermute | solution.py:13
  387.5 99.0 %all-gather.14.cloned.1.call-done = bf16[64,60,512]{2,1,0:T(8,128)(2,1)} async-done(((bf16[1,60,512]{2,1,0:T(8,128)(2,1)}), bf16[64,60,512]{2,1,0:T(8,128)(2,1)}) %all-gather.14.cloned.1.call-update) | async-done | bytes 3932176 | tf_op jit(solution)/shard_map/all_gather | solution.py:68
  486.5 6.3 %reshape.192 = bf16[3840,512]{1,0:T(8,128)(2,1)} reshape(bf16[64,60,512]{2,1,0:T(8,128)(2,1)} %all-gather.14.cloned.1.call-done) | data formatting | bytes 7864320
  492.9 5.5 %fusion.21 = bf16[512,512]{0,1:T(8,128)(2,1)S(1)} fusion(bf16[512,3840]{0,1:T(8,128)(2,1)} %all-gather.8.cloned.1.call-done, bf16[3840,512]{1,0:T(8,128)(2,1)} %reshape.192), kind=kOutput, calls=%fused_computation.21 | convolution fusion | flops 2013790208 | bytes 8388608 | tf_op jit(solution)/shard_map/dot_general | solution.py:22
  498.4 1.3 fusion.3
  499.7 1.3 fusion.5
  501.0 2.5 fusion
  503.5 2.5 fusion.13
  506.1 1.1 slice_bitcast_fusion.6
  507.2 2.0 collective-permute-start.2
  509.2 2.5 collective-permute-start.3
  511.7 3.0 fusion.18
  514.6 2.0 copy.42
  516.7 3.4 collective-permute-done.2
  520.1 10.7 %collective-permute-done.3 = f32[512,256]{0,1:T(8,128)S(1)} collective-permute-done((f32[512,256]{0,1:T(8,128)}, f32[512,256]{0,1:T(8,128)S(1)}, u32[]{:S(2)}, u32[]{:S(2)}) %collective-permute-start.3) | collective-permute-done | bytes 524320 | tf_op jit(solution)/shard_map/ppermute | solution.py:13
  530.8 1.2 fusion.28
  531.9 0.8 copy.43
  (21 shorter events, 2.1 us)
Async XLA Ops:
  7.2 123.5 %all-gather.10.cloned.1.call-start = ((), (), s32[]{:S(2)}) async-start(), calls=%async_computation.1 | async-start | bytes 2129920 | tf_op jit(solution)/shard_map/all_gather | solution.py:69
  7.9 240.8 %all-gather.12.cloned.1.call-start = ((), (), s32[]{:S(2)}) async-start(), calls=%async_computation.2 | async-start | bytes 2129920 | tf_op jit(solution)/shard_map/all_gather | solution.py:70
  8.6 351.9 %all-gather.8.cloned.1.call-start = ((), (), s32[]{:S(2)}) async-start(), calls=%async_computation | async-start | bytes 4423680 | tf_op jit(solution)/shard_map/all_gather | solution.py:60
  9.4 477.2 %all-gather.14.cloned.1.call-start = ((), (), s32[]{:S(2)}) async-start(), calls=%async_computation.3 | async-start | bytes 4259840 | tf_op jit(solution)/shard_map/all_gather | solution.py:68
  360.6 3.5 copy-start
  360.6 3.9 copy-start.2
  365.7 15.5 %collective-permute-start.1 = (bf16[512,512]{0,1:T(8,128)(2,1)S(1)}, bf16[512,512]{0,1:T(8,128)(2,1)S(1)}, u32[]{:S(2)}, u32[]{:S(2)}) collective-permute-start(bf16[512,512]{0,1:T(8,128)(2,1)S(1)} %pad_maximum_fusion), channel_id=1, source_target_pairs={{0,8},{8,16},{16,24},{24,32},{32,40},{40,48},{48,56},{56,64},{64,7... | collective-permute-start | bytes 1572872 | tf_op jit(solution)/shard_map/ppermute | solution.py:13
  367.6 19.8 %collective-permute-start = (bf16[512,512]{0,1:T(8,128)(2,1)S(1)}, bf16[512,512]{0,1:T(8,128)(2,1)S(1)}, u32[]{:S(2)}, u32[]{:S(2)}) collective-permute-start(bf16[512,512]{0,1:T(8,128)(2,1)S(1)} %pad_maximum_fusion), channel_id=1, source_target_pairs={{0,16},{8,24},{16,32},{24,40},{32,48},{40,56},{48,64},{56,72},{64,... | collective-permute-start | bytes 1572872 | tf_op jit(solution)/shard_map/ppermute | solution.py:13
  499.7 1.3 copy-start.3
  506.1 8.5 %copy-start.1 = (f32[1536,1,256]{0,2,1:T(8,128)}, f32[1536,1,256]{0,2,1:T(8,128)S(1)}, u32[]{:S(2)}) copy-start(f32[1536,1,256]{0,2,1:T(8,128)S(1)} %fusion.13) | copy-start | bytes 4718596
  507.2 12.9 %collective-permute-start.2 = (f32[512,256]{0,1:T(8,128)}, f32[512,256]{0,1:T(8,128)S(1)}, u32[]{:S(2)}, u32[]{:S(2)}) collective-permute-start(f32[512,256]{0,1:T(8,128)} %get-tuple-element.10), channel_id=1, source_target_pairs={{8,0},{16,8},{24,16},{32,24},{40,32},{48,40},{56,48},{64,56},{72,6... | collective-permute-start | bytes 1572872 | tf_op jit(solution)/shard_map/ppermute | solution.py:13
  509.2 21.6 %collective-permute-start.3 = (f32[512,256]{0,1:T(8,128)}, f32[512,256]{0,1:T(8,128)S(1)}, u32[]{:S(2)}, u32[]{:S(2)}) collective-permute-start(f32[512,256]{0,1:T(8,128)} %get-tuple-element.11), channel_id=1, source_target_pairs={{16,0},{24,8},{32,16},{40,24},{48,32},{56,40},{64,48},{72,56},{80,... | collective-permute-start | bytes 1572872 | tf_op jit(solution)/shard_map/ppermute | solution.py:13
Sparse Core Ops, SparseCore 0:
  10.1 120.4 all-gather.9
  132.8 115.8 all-gather.11
  251.9 108.6 all-gather.7
  362.6 123.9 all-gather.13
where the time goes:
time: 540 us; the launch traced here: 539 us
  waiting for transfers between devices  472 us (87%)
  matrix products  19.5 us (4%)
  local copies, waits for them, and re-layouts  17.7 us (3%)
  between operations  13.9 us (3%)
  starting transfers between devices  11.3 us (2%)
    all_gather x1, waiting for transfers between devices, local(): key_sum = add_one(lax.all_gather(key_matrix, 'ctx', axis=0, tiled=True))  119 us
    all_gather x1, waiting for transfers between devices, local(): value_sum = add_one(lax.all_gather(value_matrix, 'ctx', axis=0, tiled=True))  116 us
    all_gather x1, waiting for transfers between devices, local(): features = lax.all_gather(tokens, 'head', axis=1, tiled=True)  108 us
    all_gather x1, waiting for transfers between devices, local(): query_sum = add_one(lax.all_gather(w_query, 'ctx', axis=0, tiled=True))  99 us
    ppermute x4, waiting for transfers between devices, from_behind(): return lax.ppermute(block, axis, route)  27.9 us
    unnamed x13, local copies, waits for them, and re-layouts  15.9 us
    ppermute x4, starting transfers between devices, from_behind(): return lax.ppermute(block, axis, route)  11.1 us
  transfers between devices with their start and end apart: 8, of which 8 were waited for; matrix products, arithmetic and copies ran while one was open for 4% of the time, Pallas kernels for 0%

commit v1 on v0

--- a/solution.py
+++ b/solution.py
@@ -65,7 +65,11 @@
     def add_one(piece):
         return add_rows(features, piece)
 
-    query_sum = add_one(lax.all_gather(w_query, "ctx", axis=0, tiled=True))
+    query_sum = add_one(
+        jnp.concatenate(
+            lax.all_to_all(jnp.stack([w_query] * lax.axis_size("ctx")), "ctx", 0, 0), axis=0
+        )
+    )
     key_sum = add_one(lax.all_gather(key_matrix, "ctx", axis=0, tiled=True))
     value_sum = add_one(lax.all_gather(value_matrix, "ctx", axis=0, tiled=True))
     query = (query_sum * 0.0625).astype(jnp.bfloat16)

time: 540 us -> 505 us (0.935)
  the two profiles are of different devices: /device:TPU:24 before, /device:TPU:56 now
where the time goes in v1:
time: 505 us; the launch traced here: 504 us
  waiting for transfers between devices  420 us (83%)
  starting transfers between devices  26.5 us (5%)
  local copies, waits for them, and re-layouts  20.5 us (4%)
  matrix products  19.5 us (4%)
  between operations  13.9 us (3%)
    all_gather x1, waiting for transfers between devices, local(): key_sum = add_one(lax.all_gather(key_matrix, 'ctx', axis=0, tiled=True))  168 us
    all_gather x1, waiting for transfers between devices, local(): value_sum = add_one(lax.all_gather(value_matrix, 'ctx', axis=0, tiled=True))  115 us
    all_gather x1, waiting for transfers between devices, local(): features = lax.all_gather(tokens, 'head', axis=1, tiled=True)  108 us
    ppermute x4, waiting for transfers between devices, from_behind(): return lax.ppermute(block, axis, route)  26.3 us
    ppermute x4, starting transfers between devices, from_behind(): return lax.ppermute(block, axis, route)  13.2 us
    all_to_all x1, starting transfers between devices, local(): lax.all_to_all(jnp.stack([w_query] * lax.axis_size('ctx')), 'ctx', 0, 0)  13.2 us
    dot_general x3, matrix products, add_rows(): return jnp.dot(features, piece, preferred_element_type=jnp.float32)  10.3 us
  transfers between devices with their start and end apart: 8, of which 7 were waited for; matrix products, arithmetic and copies ran while one was open for 4% of the time, Pallas kernels for 0%

profile of v1, /device:TPU:56, one launch (start us, length us, event | category | flops | bytes accessed | tf_op | source)
XLA Modules:
  0.0 504.2 jit_solution(16954440286603299921)
XLA Ops:
  7.2 0.7 all-gather.8.cloned.1.call-update
  7.9 0.7 all-gather.10.cloned.1.call-update
  8.7 0.7 all-gather.6.cloned.1.call-update
  9.4 3.3 stack.2
  12.7 13.2 %all-to-all-start = ((bf16[64,60,512]{2,1,0:T(8,128)(2,1)}), bf16[64,60,512]{2,1,0:T(8,128)(2,1)}, u32[]{:S(2)}, u32[]{:S(2)}) async-start(bf16[64,60,512]{2,1,0:T(8,128)(2,1)} %stack.2), calls=%async_computation | async-start | bytes 8388608 | tf_op jit(solution)/shard_map/all_to_all | solution.py:70
  26.3 168.2 %all-gather.8.cloned.1.call-done = bf16[64,60,256]{2,1,0:T(8,128)(2,1)} async-done(((bf16[1,60,256]{2,1,0:T(8,128)(2,1)}), bf16[64,60,256]{2,1,0:T(8,128)(2,1)}) %all-gather.8.cloned.1.call-update) | async-done | bytes 1966096 | tf_op jit(solution)/shard_map/all_gather | solution.py:73
  194.5 2.5 reshape.194
  197.0 115.1 %all-gather.10.cloned.1.call-done = bf16[64,60,256]{2,1,0:T(8,128)(2,1)} async-done(((bf16[1,60,256]{2,1,0:T(8,128)(2,1)}), bf16[64,60,256]{2,1,0:T(8,128)(2,1)}) %all-gather.10.cloned.1.call-update) | async-done | bytes 1966096 | tf_op jit(solution)/shard_map/all_gather | solution.py:74
  312.1 3.8 reshape.196
  315.9 108.0 %all-gather.6.cloned.1.call-done = bf16[512,3840]{0,1:T(8,128)(2,1)} async-done(((bf16[512,480]{0,1:T(8,128)(2,1)}), bf16[512,3840]{0,1:T(8,128)(2,1)}) %all-gather.6.cloned.1.call-update) | async-done | bytes 3932176 | tf_op jit(solution)/shard_map/all_gather | solution.py:60
  423.9 3.5 convolution_convert_fusion.1
  427.8 1.2 convolution_convert_fusion
  429.1 1.9 collective-permute-start.1
  431.0 2.1 collective-permute-start
  433.1 1.2 compare_and_fusion
  434.3 8.4 %collective-permute-done.1 = bf16[512,512]{0,1:T(8,128)(2,1)S(1)} collective-permute-done((bf16[512,512]{0,1:T(8,128)(2,1)S(1)}, bf16[512,512]{0,1:T(8,128)(2,1)S(1)}, u32[]{:S(2)}, u32[]{:S(2)}) %collective-permute-start.1) | collective-permute-done | bytes 524320 | tf_op jit(solution)/shard_map/ppermute | solution.py:13
  442.7 5.0 collective-permute-done
  447.8 6.4 %reshape.187 = bf16[3840,512]{1,0:T(8,128)(2,1)} reshape(bf16[64,60,512]{2,1,0:T(8,128)(2,1)} %all-to-all-done) | data formatting | bytes 7864320 | tf_op jit(solution)/shard_map/reshape | solution.py:69
  454.2 5.5 %fusion.21 = bf16[512,512]{0,1:T(8,128)(2,1)S(1)} fusion(bf16[512,3840]{0,1:T(8,128)(2,1)} %all-gather.6.cloned.1.call-done, bf16[3840,512]{1,0:T(8,128)(2,1)} %reshape.187), kind=kOutput, calls=%fused_computation.21 | convolution fusion | flops 2013790208 | bytes 8388608 | tf_op jit(solution)/shard_map/dot_general | solution.py:22
  459.8 1.3 fusion.3
  461.0 1.3 fusion.5
  462.4 2.5 fusion
  464.9 2.5 fusion.13
  467.4 1.1 slice_bitcast_fusion.6
  468.6 5.9 %collective-permute-start.2 = (f32[512,256]{0,1:T(8,128)}, f32[512,256]{0,1:T(8,128)S(1)}, u32[]{:S(2)}, u32[]{:S(2)}) collective-permute-start(f32[512,256]{0,1:T(8,128)} %get-tuple-element.10), channel_id=1, source_target_pairs={{8,0},{16,8},{24,16},{32,24},{40,32},{48,40},{56,48},{64,56},{72,6... | collective-permute-start | bytes 1572872 | tf_op jit(solution)/shard_map/ppermute | solution.py:13
  474.4 3.4 collective-permute-start.3
  477.8 3.0 fusion.18
  480.7 2.0 copy.42
  482.8 2.9 collective-permute-done.2
  485.7 10.0 %collective-permute-done.3 = f32[512,256]{0,1:T(8,128)S(1)} collective-permute-done((f32[512,256]{0,1:T(8,128)}, f32[512,256]{0,1:T(8,128)S(1)}, u32[]{:S(2)}, u32[]{:S(2)}) %collective-permute-start.3) | collective-permute-done | bytes 524320 | tf_op jit(solution)/shard_map/ppermute | solution.py:13
  495.7 1.2 fusion.28
  496.9 0.8 copy.43
  (23 shorter events, 1.0 us)
Async XLA Ops:
  7.2 187.3 %all-gather.8.cloned.1.call-start = ((), (), s32[]{:S(2)}) async-start(), calls=%async_computation.2 | async-start | bytes 2129920 | tf_op jit(solution)/shard_map/all_gather | solution.py:73
  7.9 304.2 %all-gather.10.cloned.1.call-start = ((), (), s32[]{:S(2)}) async-start(), calls=%async_computation.3 | async-start | bytes 2129920 | tf_op jit(solution)/shard_map/all_gather | solution.py:74
  8.6 415.3 %all-gather.6.cloned.1.call-start = ((), (), s32[]{:S(2)}) async-start(), calls=%async_computation.1 | async-start | bytes 4423680 | tf_op jit(solution)/shard_map/all_gather | solution.py:60
  12.7 13.2 %copy-start.2 = (s32[32]{0:T(128)S(1)}, s32[32]{0:T(128)}, u32[]{:S(2)}) copy-start(s32[32]{0:T(128)} %param.11) | copy-start | bytes 388
  12.7 435.1 %all-to-all-start = ((bf16[64,60,512]{2,1,0:T(8,128)(2,1)}), bf16[64,60,512]{2,1,0:T(8,128)(2,1)}, u32[]{:S(2)}, u32[]{:S(2)}) async-start(bf16[64,60,512]{2,1,0:T(8,128)(2,1)} %stack.2), calls=%async_computation | async-start | bytes 8388608 | tf_op jit(solution)/shard_map/all_to_all | solution.py:70
  423.9 3.5 copy-start
  423.9 3.9 copy-start.3
  429.1 13.6 %collective-permute-start.1 = (bf16[512,512]{0,1:T(8,128)(2,1)S(1)}, bf16[512,512]{0,1:T(8,128)(2,1)S(1)}, u32[]{:S(2)}, u32[]{:S(2)}) collective-permute-start(bf16[512,512]{0,1:T(8,128)(2,1)S(1)} %pad_maximum_fusion), channel_id=1, source_target_pairs={{0,8},{8,16},{16,24},{24,32},{32,40},{40,48},{48,56},{56,64},{64,7... | collective-permute-start | bytes 1572872 | tf_op jit(solution)/shard_map/ppermute | solution.py:13
  431.0 16.7 %collective-permute-start = (bf16[512,512]{0,1:T(8,128)(2,1)S(1)}, bf16[512,512]{0,1:T(8,128)(2,1)S(1)}, u32[]{:S(2)}, u32[]{:S(2)}) collective-permute-start(bf16[512,512]{0,1:T(8,128)(2,1)S(1)} %pad_maximum_fusion), channel_id=1, source_target_pairs={{0,16},{8,24},{16,32},{24,40},{32,48},{40,56},{48,64},{56,72},{64,... | collective-permute-start | bytes 1572872 | tf_op jit(solution)/shard_map/ppermute | solution.py:13
  461.0 1.3 copy-start.4
  467.4 13.3 %copy-start.1 = (f32[1536,1,256]{0,2,1:T(8,128)}, f32[1536,1,256]{0,2,1:T(8,128)S(1)}, u32[]{:S(2)}) copy-start(f32[1536,1,256]{0,2,1:T(8,128)S(1)} %fusion.13) | copy-start | bytes 4718596
  468.6 17.1 %collective-permute-start.2 = (f32[512,256]{0,1:T(8,128)}, f32[512,256]{0,1:T(8,128)S(1)}, u32[]{:S(2)}, u32[]{:S(2)}) collective-permute-start(f32[512,256]{0,1:T(8,128)} %get-tuple-element.10), channel_id=1, source_target_pairs={{8,0},{16,8},{24,16},{32,24},{40,32},{48,40},{56,48},{64,56},{72,6... | collective-permute-start | bytes 1572872 | tf_op jit(solution)/shard_map/ppermute | solution.py:13
  474.4 21.3 %collective-permute-start.3 = (f32[512,256]{0,1:T(8,128)}, f32[512,256]{0,1:T(8,128)S(1)}, u32[]{:S(2)}, u32[]{:S(2)}) collective-permute-start(f32[512,256]{0,1:T(8,128)} %get-tuple-element.11), channel_id=1, source_target_pairs={{16,0},{24,8},{32,16},{40,24},{48,32},{56,40},{64,48},{72,56},{80,... | collective-permute-start | bytes 1572872 | tf_op jit(solution)/shard_map/ppermute | solution.py:13
Sparse Core Ops, SparseCore 0:
  10.1 184.3 all-gather.7
  196.7 115.4 all-gather.9
  315.3 108.5 all-gather.5
